TPU v7x, 32 devices: a whole 2x2x4 slice. The times are simulated.
32 devices in a mesh: slab: 8 (over z, core), grp: 4 (over y, x).
Axes of the slice: x: 2, y: 2, z: 4, core: 2. Of those that a mesh axis runs over, the one named last changes fastest.
Arguments:
- stress: bfloat16 [6, 262144], P(None, ('slab', 'grp')), may hold values from -6 to 6
- interp_weight: bfloat16 [2048, 64, 128], P(('slab', 'grp')), may hold values from -0.5 to 0.5
- block_owner: int32 [2048, 1], P(('slab', 'grp')), may hold values from 0 to 3; in each aligned block of 64 rows (0 to 63, 64 to 127, ...) at most 48 rows name the same one
- block_local: int32 [2048], P(('slab', 'grp')), may hold values from 0 to 63
- slip_system: int32 [131072], P(('slab', 'grp')), may hold values from 0 to 11
- mobility: float32 [131072], P(('slab', 'grp')), may hold values from 0.3 to 3
- position: float32 [3, 131072], P(None, ('slab', 'grp')), may hold values from -6 to 6
- target_slab: int32 [131072, 1], P(('slab', 'grp')), may hold values from 0 to 7; in each aligned block of 4096 rows (0 to 4095, 4096 to 8191, ...) at most 1024 rows name the same one
Outputs:
- distortion: float32 [6, 262144], P(None, ('slab', 'grp'))
- arrived: float32 [4, 262144], P(None, ('slab', 'grp'))
Inputs may be any that keep to these rules, and one draw needn't show every extreme that they name: Among the 64 segment blocks of one device at most 48 have the same block_owner; on some device exactly 48 do. Among the 4096 segments of one device at most 1024 have the same target_slab; on some device exactly 1024 do.
All inputs are finite; a program needn't handle non-finite values.
Results may differ from a plain program's by a relative error of at most 0.01.
Values may be sent and summed in bfloat16 or wider, within the bound.
No kernel may reach another device: no remote copies, remote signals or barrier semaphores. Data moves between devices by JAX's collectives and lax.ppermute only.
A program may use at most 64 MiB of HBM per device.

v0:
```python
import jax
import jax.numpy as jnp
import numpy as np
from jax import lax
from jax.sharding import PartitionSpec as P

NC = 6
NSYS = 12
BLK = 128
SEGB = 64
glide_time = 0.5


def slip_tables():
    normal_list = [(1.0, 1.0, 1.0), (-1.0, 1.0, 1.0), (1.0, -1.0, 1.0), (1.0, 1.0, -1.0)]
    schmid_rows = []
    glide_rows = []
    for along_x, along_y, along_z in normal_list:
        normal_vec = np.array([along_x, along_y, along_z]) / np.sqrt(3.0)
        for burgers in (
            (along_y, -along_x, 0.0),
            (along_z, 0.0, -along_x),
            (0.0, along_z, -along_y),
        ):
            burgers_vec = np.array(burgers) / np.sqrt(2.0)
            tensor = 0.5 * (np.outer(normal_vec, burgers_vec) + np.outer(burgers_vec, normal_vec))
            schmid_rows.append(
                [
                    tensor[0, 0],
                    tensor[1, 1],
                    tensor[2, 2],
                    2.0 * tensor[1, 2],
                    2.0 * tensor[0, 2],
                    2.0 * tensor[0, 1],
                ]
            )
            glide_rows.append(burgers_vec)
    return (np.array(schmid_rows, np.float32).T, np.array(glide_rows, np.float32).T)


def slot_ranks(labels, count):
    onehot = (labels[:, None] == jnp.arange(count, dtype=jnp.int32)[None, :]).astype(jnp.int32)
    return jnp.sum((jnp.cumsum(onehot, axis=0) - onehot) * onehot, axis=1)


def body(
    stress, interp_weight, block_owner, block_local, slip_system, mobility, position, target_slab
):
    schmid_np, glide_np = slip_tables()
    schmid = jnp.asarray(schmid_np, jnp.float32)
    glide_table = jnp.asarray(glide_np, jnp.float32)
    group_size = lax.axis_size("grp")
    slab_count = lax.axis_size("slab")
    block_count = interp_weight.shape[0]
    local_blocks = stress.shape[1] // BLK
    owner_index = block_owner[:, 0]
    slab_stress = lax.all_gather(stress, "grp", axis=1, tiled=True)
    stress_tiles = slab_stress.reshape(NC, group_size * local_blocks, BLK)[
        :, owner_index * local_blocks + block_local, :
    ]
    sampled = jnp.einsum(
        "cbv,bsv->cbs", stress_tiles, interp_weight, preferred_element_type=jnp.float32
    ).reshape(NC, -1)
    systems_hot = (jnp.arange(NSYS, dtype=jnp.int32)[:, None] == slip_system[None, :]).astype(
        jnp.float32
    )
    factors = jnp.dot(schmid, systems_hot, precision=lax.Precision.HIGHEST)
    resolved = jnp.sum(factors * sampled, axis=0)
    glide_step = glide_time * mobility * resolved
    weight_term = (
        (glide_step[None, :] * factors).astype(jnp.bfloat16).reshape(NC, block_count, SEGB)
    )
    spread = jnp.einsum(
        "cbs,bsv->cbv", weight_term, interp_weight, preferred_element_type=jnp.float32
    )
    dense_term = (
        jnp.zeros((NC, group_size * local_blocks, BLK), jnp.float32)
        .at[:, owner_index * local_blocks + block_local, :]
        .add(spread)
    )
    distortion = lax.psum_scatter(
        dense_term.reshape(NC, -1).astype(jnp.bfloat16), "grp", scatter_dimension=1, tiled=True
    ).astype(jnp.float32)
    glide_dirs = jnp.dot(glide_table, systems_hot, precision=lax.Precision.HIGHEST)
    moved_position = position + glide_dirs * glide_step[None, :]
    payload = jnp.concatenate([moved_position, glide_step[None, :]], axis=0)
    target = target_slab[:, 0]
    target_rank = slot_ranks(target, slab_count)
    per_peer = 2 * payload.shape[1] // slab_count
    outgoing_moves = (
        jnp.zeros((4, slab_count, per_peer), jnp.float32).at[:, target, target_rank].set(payload)
    )
    arrived = (
        lax.all_to_all(
            outgoing_moves.astype(jnp.bfloat16), "slab", split_axis=1, concat_axis=1, tiled=True
        )
        .astype(outgoing_moves.dtype)
        .reshape(4, -1)
    )
    return (distortion, arrived)


def solution(mesh):
    placed = (
        P(None, ("slab", "grp")),
        P(("slab", "grp"), None, None),
        P(("slab", "grp"), None),
        P(("slab", "grp")),
        P(("slab", "grp")),
        P(("slab", "grp")),
        P(None, ("slab", "grp")),
        P(("slab", "grp"), None),
    )
    return jax.shard_map(
        body,
        mesh=mesh,
        in_specs=placed,
        out_specs=(P(None, ("slab", "grp")), P(None, ("slab", "grp"))),
        check_vma=False,
    )
```

profile of v0, /device:TPU:0, one launch (start us, length us, event | category | flops | bytes accessed | tf_op | source)
XLA Modules:
  0.0 67.4 jit_solution(1898360276803271494)
XLA Ops:
  7.2 0.8 %compare_select_fusion.2 = s32[64]{0:T(128)S(1)} fusion(s32[64]{0:T(128)} %param.13, s32[64,1]{0,1:T(1,128)} %param.12), kind=kLoop, calls=%fused_computation.37 | loop fusion | flops 320 | bytes 768 | tf_op jit(solution)/shard_map/select_n | solution.py:79
  8.0 11.8 %all_gather.3 = bf16[6,32768]{1,0:T(8,128)(2,1)S(1)} all-gather(bf16[6,8192]{1,0:T(8,128)(2,1)} %param.10), channel_id=1, replica_groups=mesh['slab'=8,'grp'=4] {'grp'}, dimensions={1}, use_global_device_ids=true | all-gather | bytes 491520 | tf_op jit(solution)/shard_map/all_gather | solution.py:57
  19.8 0.6 gather_fusion
  20.5 0.6 convolution_bitcast_fusion
  21.3 1.0 %multiply_reduce_fusion = (f32[4096]{0:T(1024)S(1)}, f32[6,4096]{1,0:T(8,128)S(1)}) fusion(f32[6,4096]{1,0:T(8,128)S(1)} %reshape.55, f32[6,12]{1,0:T(8,128)} %constant.7.clone, s32[4096]{0:T(1024)} %param.14), kind=kOutput, calls=%fused_computation.24 | convolution fusion | flops 3633152 | bytes 229664 | tf_op jit(solution)/shard_map/dot_general | solution.py:67
  22.3 0.7 %multiply_multiply_fusion = f32[4096]{0:T(1024)S(1)} fusion(f32[4096]{0:T(1024)S(1)} %get-tuple-element.2, f32[4096]{0:T(1024)} %param.15), kind=kLoop, calls=%fused_computation.34 | loop fusion | flops 8192 | bytes 49152 | tf_op jit(solution)/shard_map/mul | solution.py:69
  23.2 0.4 fusion.9
  23.6 2.7 %scatter_fusion = f32[6,256,128]{2,0,1:T(8,128)S(1)} fusion(f32[6,256,128]{2,0,1:T(8,128)S(1)} %broadcast_in_dim.8, s32[64]{0:T(128)S(1)} %compare_select_fusion.2, f32[64,6,128]{2,1,0:T(8,128)S(1)} %fusion.9), kind=kCustom, calls=%fused_computation.1 | custom fusion | flops 49152 | bytes 590080 | tf_op jit(solution)/shard_map/scatter-add | solution.py:79
  26.4 0.9 %convert_bitcast_fusion = bf16[6,32768]{1,0:T(8,128)(2,1)} fusion(f32[6,256,128]{2,0,1:T(8,128)S(1)} %scatter_fusion), kind=kLoop, calls=%fused_computation.9 | loop fusion | flops 196608 | bytes 1179648 | tf_op jit(solution)/shard_map/convert_element_type | solution.py:82
  27.3 2.3 %reduce-window.6 = s32[8,32,128]{2,1,0:T(8,128)S(1)} reduce-window(s32[8,32,128]{2,1,0:T(8,128)S(1)} %fusion.13, s32[]{:T(128)} %constant.11.clone.1), window={size=1x1x128 pad=0_0x0_0x127_0}, to_apply=%region_3.0 | reduce-window | flops 4161536 | bytes 262148 | tf_op jit(solution)/shard_map/reduce-window
  29.6 0.3 slice_reduce_fusion
  29.9 0.2 reduce-window.9
  30.1 0.1 add_bitcast_fusion
  30.2 0.1 fusion.7
  30.4 0.2 fusion.1
  30.7 0.6 copy.22
  31.3 0.1 multiply_reduce_fusion.1
  31.4 0.1 and_reduce_fusion
  31.6 12.8 %scatter_custom_fusion.1 = f32[4,8192]{0,1:T(8,128)} fusion(s32[4096]{0:T(1024)S(1)} %broadcast_select_fusion, f32[4096,4]{1,0:T(8,128)S(1)} %copy.22, f32[]{:T(128)} %constant.9.clone.1), kind=kCustom, calls=%fused_computation.6 | custom fusion | bytes 131076
  44.3 2.4 %convert_element_type.31 = bf16[4,8192]{0,1:T(8,128)(2,1)S(1)} convert(f32[4,8192]{0,1:T(8,128)} %scatter_custom_fusion.1) | non-fusion elementwise | flops 32768 | bytes 196608 | tf_op jit(solution)/shard_map/convert_element_type | solution.py:95
  46.7 0.9 %copy.23 = bf16[4,8,1024]{2,0,1:T(4,128)(2,1)S(1)} copy(bf16[4,8,1024]{0,2,1:T(8,128)(2,1)S(1)} %bitcast.48) | data formatting | bytes 131072 | tf_op jit(solution)/shard_map/convert_element_type | solution.py:95
  47.6 10.6 %all_to_all.5 = bf16[4,8,1024]{2,0,1:T(4,128)(2,1)S(1)} all-to-all(bf16[4,8,1024]{2,0,1:T(4,128)(2,1)S(1)} %copy.23), channel_id=1, replica_groups=mesh['slab'=8,'grp'=4] {'slab'}, dimensions={1} | all-to-all | bytes 131072 | tf_op jit(solution)/shard_map/all_to_all | solution.py:94
  58.2 0.7 convert.1
  58.9 1.6 %convert_element_type.27 = f32[6,8192]{1,0:T(8,128)} convert(bf16[6,8192]{1,0:T(8,128)(2,1)} %reduce-scatter.2.cloned.1.call-done) | non-fusion elementwise | flops 49152 | bytes 294912 | tf_op jit(solution)/shard_map/convert_element_type | solution.py:83
  (27 shorter events, 0.5 us)
Async XLA Ops:
  7.2 13.3 %copy-start = (bf16[64,64,128]{2,1,0:T(8,128)(2,1)S(1)}, bf16[64,64,128]{2,1,0:T(8,128)(2,1)}, u32[]{:S(2)}) copy-start(bf16[64,64,128]{2,1,0:T(8,128)(2,1)} %param.11) | copy-start | bytes 3145732
  7.2 51.7 %reduce-scatter.2.cloned.1.call-start = ((), (), s32[]{:S(2)}) async-start(), calls=%async_computation.2 | async-start | bytes 655360 | tf_op jit(solution)/shard_map/reduce_scatter | solution.py:81
  20.5 6.8 %copy-start.1 = (s32[4096,1]{0,1:T(1,128)S(1)}, s32[4096,1]{0,1:T(1,128)}, u32[]{:S(2)}) copy-start(s32[4096,1]{0,1:T(1,128)} %param.17) | copy-start | bytes 49156
  21.1 9.2 %copy-start.2 = (f32[3,4096]{1,0:T(4,128)S(1)}, f32[3,4096]{1,0:T(4,128)}, u32[]{:S(2)}) copy-start(f32[3,4096]{1,0:T(4,128)} %param.16) | copy-start | bytes 147460
  21.1 9.2 %copy-start.3 = (s32[4096]{0:T(1024)S(1)}, s32[4096]{0:T(1024)}, u32[]{:S(2)}) copy-start(s32[4096]{0:T(1024)} %param.14) | copy-start | bytes 49156
  21.1 9.3 %copy-start.4 = (f32[3,12]{1,0:T(4,128)S(1)}, f32[3,12]{1,0:T(4,128)}, u32[]{:S(2)}) copy-start(f32[3,12]{1,0:T(4,128)} %constant.8.clone) | copy-start | bytes 436
  23.1 8.2 %copy-start.6 = (s32[2]{0:T(128)S(1)}, s32[2]{0:T(128)}, u32[]{:S(2)}) copy-start(s32[2]{0:T(128)} %constant.28) | copy-start | bytes 28
  23.1 8.3 %copy-start.5 = (s32[2]{0:T(128)S(1)}, s32[2]{0:T(128)}, u32[]{:S(2)}) copy-start(s32[2]{0:T(128)} %constant.31) | copy-start | bytes 28
Sparse Core Ops, SparseCore 0:
  27.4 25.0 reduce-scatter.1
where the time goes:
time: 67.8 us; the launch traced here: 67.4 us
  blocking collectives  22.4 us (33%)
  local copies, waits for them, and re-layouts  15.6 us (23%)
  between operations  14.2 us (21%)
  other arithmetic  12.8 us (19%)
  matrix products  2.21 us (3%)
    unnamed x15, local copies, waits for them, and re-layouts  12.8 us
    all_gather x1, blocking collectives, body(): slab_stress = lax.all_gather(stress, 'grp', axis=1, tiled=True)  11.8 us
    all_to_all x1, blocking collectives, body(): lax.all_to_all(outgoing_moves.astype(jnp.bfloat16), 'slab', split_axis=1,...  10.6 us
    scatter-add x1, other arithmetic, body(): dense_term = jnp.zeros((NC, group_size * local_blocks, BLK), jnp.float32)...  2.74 us
    another operation x2, other arithmetic  2.5 us
    convert_element_type x1, other arithmetic, body(): outgoing_moves.astype(jnp.bfloat16)  2.39 us
    convert_element_type x1, other arithmetic, body(): distortion = lax.psum_scatter(dense_term.reshape(NC, -1).astype(jnp.bfloa...  1.62 us
  transfers between devices with their start and end apart: 1, of which 0 were waited for; matrix products, arithmetic and copies ran while one was open for 31% of the time, Pallas kernels for 0%

commit v1 on v0

--- a/solution.py
+++ b/solution.py
@@ -9,6 +9,22 @@
 BLK = 128
 SEGB = 64
 glide_time = 0.5
+
+
+def exchange_in_pairs(array, axis, split, join):
+    ways, here = (lax.axis_size(axis), lax.axis_index(axis))
+    width = array.shape[split] // ways
+    shape = list(array.shape)
+    shape[split] = width
+    height = shape[join]
+    shape[join] = height * ways
+    full = jnp.zeros(shape, array.dtype)
+    for mask in range(ways):
+        part = lax.dynamic_slice_in_dim(array, (here ^ mask) * width, width, axis=split)
+        if mask:
+            part = lax.ppermute(part, axis, [(d, d ^ mask) for d in range(ways)])
+        full = lax.dynamic_update_slice_in_dim(full, part, (here ^ mask) * height, axis=join)
+    return full
 
 
 def slip_tables():
@@ -91,9 +107,7 @@
         jnp.zeros((4, slab_count, per_peer), jnp.float32).at[:, target, target_rank].set(payload)
     )
     arrived = (
-        lax.all_to_all(
-            outgoing_moves.astype(jnp.bfloat16), "slab", split_axis=1, concat_axis=1, tiled=True
-        )
+        exchange_in_pairs(outgoing_moves.astype(jnp.bfloat16), "slab", 1, 1)
         .astype(outgoing_moves.dtype)
         .reshape(4, -1)
     )

time: 67.8 us -> 107 us (1.58)
  the two profiles are of different devices: /device:TPU:0 before, /device:TPU:17 now
where the time goes in v1:
time: 107 us
  waiting for transfers between devices  41 us (38%)
  local copies, waits for them, and re-layouts  19.1 us (18%)
  between operations  14.4 us (13%)
  other arithmetic  12.2 us (11%)
  starting transfers between devices  9.07 us (8%)
  blocking collectives  8.95 us (8%)
  matrix products  2.21 us (2%)
    ppermute x7, waiting for transfers between devices, exchange_in_pairs(): part = lax.ppermute(part, axis, [(d, d ^ mask) for d in range(ways)])  41 us
    unnamed x16, local copies, waits for them, and re-layouts  13.5 us
    ppermute x7, starting transfers between devices, exchange_in_pairs(): part = lax.ppermute(part, axis, [(d, d ^ mask) for d in range(ways)])  9.03 us
    all_gather x1, blocking collectives, body(): slab_stress = lax.all_gather(stress, 'grp', axis=1, tiled=True)  8.95 us
    scatter-add x1, other arithmetic, body(): dense_term = jnp.zeros((NC, group_size * local_blocks, BLK), jnp.float32)...  2.73 us
    another operation x2, other arithmetic  2.5 us
    convert_element_type x1, other arithmetic, body(): outgoing_moves.astype(jnp.bfloat16)  2.39 us
  transfers between devices with their start and end apart: 8, of which 5 were waited for; matrix products, arithmetic and copies ran while one was open for 22% of the time, Pallas kernels for 0%

profile of v1, /device:TPU:17, one launch (start us, length us, event | category | flops | bytes accessed | tf_op | source)
XLA Modules:
  0.0 106.9 jit_solution(13618398128275697702)
XLA Ops:
  7.2 0.8 compare_select_fusion.2
  8.0 9.0 %all_gather.3 = bf16[6,32768]{1,0:T(8,128)(2,1)S(1)} all-gather(bf16[6,8192]{1,0:T(8,128)(2,1)} %param.10), channel_id=1, replica_groups=mesh['slab'=8,'grp'=4] {'grp'}, dimensions={1}, use_global_device_ids=true | all-gather | bytes 491520 | tf_op jit(solution)/shard_map/all_gather | solution.py:73
  16.9 0.6 gather_fusion
  17.6 0.6 convolution_bitcast_fusion
  18.4 1.0 multiply_reduce_fusion
  19.4 0.7 multiply_multiply_fusion
  20.7 2.7 %scatter_fusion = f32[6,256,128]{2,0,1:T(8,128)S(1)} fusion(f32[6,256,128]{2,0,1:T(8,128)S(1)} %broadcast_in_dim.10, s32[64]{0:T(128)S(1)} %compare_select_fusion.2, f32[64,6,128]{2,1,0:T(8,128)S(1)} %fusion.9), kind=kCustom, calls=%fused_computation.1 | custom fusion | flops 49152 | bytes 590080 | tf_op jit(solution)/shard_map/scatter-add | solution.py:95
  23.5 0.9 convert_bitcast_fusion
  24.4 2.3 %reduce-window.6 = s32[8,32,128]{2,1,0:T(8,128)S(1)} reduce-window(s32[8,32,128]{2,1,0:T(8,128)S(1)} %fusion.13, s32[]{:T(128)} %constant.21.clone.1), window={size=1x1x128 pad=0_0x0_0x127_0}, to_apply=%region_3.0 | reduce-window | flops 4161536 | bytes 262148 | tf_op jit(solution)/shard_map/reduce-window
  27.9 0.6 copy.25
  28.7 12.8 %scatter_custom_fusion.1 = f32[4,8192]{0,1:T(8,128)} fusion(s32[4096]{0:T(1024)S(1)} %broadcast_select_fusion, f32[4096,4]{1,0:T(8,128)S(1)} %copy.25, f32[]{:T(128)} %constant.19.clone.1), kind=kCustom, calls=%fused_computation.6 | custom fusion | bytes 131076
  41.5 2.4 %convert_element_type.31 = bf16[4,8192]{0,1:T(8,128)(2,1)S(1)} convert(f32[4,8192]{0,1:T(8,128)} %scatter_custom_fusion.1) | non-fusion elementwise | flops 32768 | bytes 196608 | tf_op jit(solution)/shard_map/convert_element_type | solution.py:110
  43.9 1.1 %constant_dynamic-slice_fusion = (bf16[4,1,1024]{0,2,1:T(8,128)(2,1)}, bf16[4,1,1024]{0,2,1:T(8,128)(2,1)}, bf16[4,1,1024]{0,2,1:T(8,128)(2,1)}, bf16[4,1,1024]{...) fusion(bf16[4,8,1024]{0,2,1:T(8,128)(2,1)S(1)} %bitcast.49, ...), kind=kLoop, calls=%fused_computation.39 | loop fusion | bytes 131104 | tf_op jit(solution)/shard_map/dynamic_slice | solution.py:23
  45.0 2.1 %collective-permute-start = (bf16[4,1,1024]{0,2,1:T(8,128)(2,1)S(1)}, bf16[4,1,1024]{0,2,1:T(8,128)(2,1)S(1)}, u32[]{:S(2)}, u32[]{:S(2)}) collective-permute-start(bf16[4,1,1024]{0,2,1:T(8,128)(2,1)S(1)} %get-tuple-element.8), channel_id=1, source_target_pairs={{0,4},{4,0},{8,12},{12,8},{16,20},{20,16},{24,28},{28,24},{1,5},{5... | collective-permute-start | bytes 24584 | tf_op jit(solution)/shard_map/ppermute | solution.py:25
  47.1 1.3 %collective-permute-start.1 = (bf16[4,1,1024]{0,2,1:T(8,128)(2,1)S(1)}, bf16[4,1,1024]{0,2,1:T(8,128)(2,1)S(1)}, u32[]{:S(2)}, u32[]{:S(2)}) collective-permute-start(bf16[4,1,1024]{0,2,1:T(8,128)(2,1)S(1)} %get-tuple-element.7), channel_id=1, source_target_pairs={{0,8},{4,12},{8,0},{12,4},{16,24},{20,28},{24,16},{28,20},{1,9},{5... | collective-permute-start | bytes 24584 | tf_op jit(solution)/shard_map/ppermute | solution.py:25
  48.8 2.7 %collective-permute-start.4 = (bf16[4,1,1024]{0,2,1:T(8,128)(2,1)}, bf16[4,1,1024]{0,2,1:T(8,128)(2,1)S(1)}, u32[]{:S(2)}, u32[]{:S(2)}) collective-permute-start(bf16[4,1,1024]{0,2,1:T(8,128)(2,1)} %get-tuple-element.4), channel_id=1, source_target_pairs={{0,20},{4,16},{8,28},{12,24},{16,4},{20,0},{24,12},{28,8},{1,21},{... | collective-permute-start | bytes 24584 | tf_op jit(solution)/shard_map/ppermute | solution.py:25
  51.7 10.8 %collective-permute-done.1 = bf16[4,1,1024]{0,2,1:T(8,128)(2,1)S(1)} collective-permute-done((bf16[4,1,1024]{0,2,1:T(8,128)(2,1)S(1)}, bf16[4,1,1024]{0,2,1:T(8,128)(2,1)S(1)}, u32[]{:S(2)}, u32[]{:S(2)}) %collective-permute-start.1) | collective-permute-done | bytes 8224 | tf_op jit(solution)/shard_map/ppermute | solution.py:25
  62.5 2.3 %collective-permute-start.6 = (bf16[4,1,1024]{0,2,1:T(8,128)(2,1)}, bf16[4,1,1024]{0,2,1:T(8,128)(2,1)S(1)}, u32[]{:S(2)}, u32[]{:S(2)}) collective-permute-start(bf16[4,1,1024]{0,2,1:T(8,128)(2,1)} %get-tuple-element.2), channel_id=1, source_target_pairs={{0,28},{4,24},{8,20},{12,16},{16,12},{20,8},{24,4},{28,0},{1,29},{... | collective-permute-start | bytes 24584 | tf_op jit(solution)/shard_map/ppermute | solution.py:25
  65.8 2.4 %collective-permute-done.2 = bf16[4,1,1024]{0,2,1:T(8,128)(2,1)S(1)} collective-permute-done((bf16[4,1,1024]{0,2,1:T(8,128)(2,1)}, bf16[4,1,1024]{0,2,1:T(8,128)(2,1)S(1)}, u32[]{:S(2)}, u32[]{:S(2)}) %collective-permute-start.2) | collective-permute-done | bytes 8224 | tf_op jit(solution)/shard_map/ppermute | solution.py:25
  68.8 3.5 %collective-permute-done.4 = bf16[4,1,1024]{0,2,1:T(8,128)(2,1)S(1)} collective-permute-done((bf16[4,1,1024]{0,2,1:T(8,128)(2,1)}, bf16[4,1,1024]{0,2,1:T(8,128)(2,1)S(1)}, u32[]{:S(2)}, u32[]{:S(2)}) %collective-permute-start.4) | collective-permute-done | bytes 8224 | tf_op jit(solution)/shard_map/ppermute | solution.py:25
  72.7 18.7 %collective-permute-done.5 = bf16[4,1,1024]{0,2,1:T(8,128)(2,1)S(1)} collective-permute-done((bf16[4,1,1024]{0,2,1:T(8,128)(2,1)}, bf16[4,1,1024]{0,2,1:T(8,128)(2,1)S(1)}, u32[]{:S(2)}, u32[]{:S(2)}) %collective-permute-start.5) | collective-permute-done | bytes 8224 | tf_op jit(solution)/shard_map/ppermute | solution.py:25
  91.7 5.6 %collective-permute-done.6 = bf16[4,1,1024]{0,2,1:T(8,128)(2,1)S(1)} collective-permute-done((bf16[4,1,1024]{0,2,1:T(8,128)(2,1)}, bf16[4,1,1024]{0,2,1:T(8,128)(2,1)S(1)}, u32[]{:S(2)}, u32[]{:S(2)}) %collective-permute-start.6) | collective-permute-done | bytes 8224 | tf_op jit(solution)/shard_map/ppermute | solution.py:25
  97.7 0.7 copy.35
  98.5 1.6 %convert_element_type.27 = f32[6,8192]{1,0:T(8,128)} convert(bf16[6,8192]{1,0:T(8,128)(2,1)} %reduce-scatter.2.cloned.1.call-done) | non-fusion elementwise | flops 49152 | bytes 294912 | tf_op jit(solution)/shard_map/convert_element_type | solution.py:99
  (58 shorter events, 5.2 us)
Async XLA Ops:
  7.2 10.4 %copy-start = (bf16[64,64,128]{2,1,0:T(8,128)(2,1)S(1)}, bf16[64,64,128]{2,1,0:T(8,128)(2,1)}, u32[]{:S(2)}) copy-start(bf16[64,64,128]{2,1,0:T(8,128)(2,1)} %param.11) | copy-start | bytes 3145732
  7.2 91.3 %reduce-scatter.2.cloned.1.call-start = ((), (), s32[]{:S(2)}) async-start(), calls=%async_computation.1 | async-start | bytes 655360 | tf_op jit(solution)/shard_map/reduce_scatter | solution.py:97
  17.6 6.8 %copy-start.1 = (s32[4096,1]{0,1:T(1,128)S(1)}, s32[4096,1]{0,1:T(1,128)}, u32[]{:S(2)}) copy-start(s32[4096,1]{0,1:T(1,128)} %param.17) | copy-start | bytes 49156
  18.2 9.2 %copy-start.2 = (f32[3,4096]{1,0:T(4,128)S(1)}, f32[3,4096]{1,0:T(4,128)}, u32[]{:S(2)}) copy-start(f32[3,4096]{1,0:T(4,128)} %param.16) | copy-start | bytes 147460
  18.2 9.2 %copy-start.3 = (s32[4096]{0:T(1024)S(1)}, s32[4096]{0:T(1024)}, u32[]{:S(2)}) copy-start(s32[4096]{0:T(1024)} %param.14) | copy-start | bytes 49156
  18.2 9.2 %copy-start.4 = (f32[3,12]{1,0:T(4,128)S(1)}, f32[3,12]{1,0:T(4,128)}, u32[]{:S(2)}) copy-start(f32[3,12]{1,0:T(4,128)} %constant.50.clone) | copy-start | bytes 436
  18.2 9.5 %copy-start.6 = (s32[2]{0:T(128)S(1)}, s32[2]{0:T(128)}, u32[]{:S(2)}) copy-start(s32[2]{0:T(128)} %constant.51) | copy-start | bytes 28
  20.2 8.3 %copy-start.5 = (s32[2]{0:T(128)S(1)}, s32[2]{0:T(128)}, u32[]{:S(2)}) copy-start(s32[2]{0:T(128)} %constant.54) | copy-start | bytes 28
  45.0 6.5 %collective-permute-start = (bf16[4,1,1024]{0,2,1:T(8,128)(2,1)S(1)}, bf16[4,1,1024]{0,2,1:T(8,128)(2,1)S(1)}, u32[]{:S(2)}, u32[]{:S(2)}) collective-permute-start(bf16[4,1,1024]{0,2,1:T(8,128)(2,1)S(1)} %get-tuple-element.8), channel_id=1, source_target_pairs={{0,4},{4,0},{8,12},{12,8},{16,20},{20,16},{24,28},{28,24},{1,5},{5... | collective-permute-start | bytes 24584 | tf_op jit(solution)/shard_map/ppermute | solution.py:25
  47.1 15.4 %collective-permute-start.1 = (bf16[4,1,1024]{0,2,1:T(8,128)(2,1)S(1)}, bf16[4,1,1024]{0,2,1:T(8,128)(2,1)S(1)}, u32[]{:S(2)}, u32[]{:S(2)}) collective-permute-start(bf16[4,1,1024]{0,2,1:T(8,128)(2,1)S(1)} %get-tuple-element.7), channel_id=1, source_target_pairs={{0,8},{4,12},{8,0},{12,4},{16,24},{20,28},{24,16},{28,20},{1,9},{5... | collective-permute-start | bytes 24584 | tf_op jit(solution)/shard_map/ppermute | solution.py:25
  48.4 19.8 %collective-permute-start.2 = (bf16[4,1,1024]{0,2,1:T(8,128)(2,1)}, bf16[4,1,1024]{0,2,1:T(8,128)(2,1)S(1)}, u32[]{:S(2)}, u32[]{:S(2)}) collective-permute-start(bf16[4,1,1024]{0,2,1:T(8,128)(2,1)} %get-tuple-element.6), channel_id=1, source_target_pairs={{0,12},{4,8},{8,4},{12,0},{16,28},{20,24},{24,20},{28,16},{1,13},{... | collective-permute-start | bytes 24584 | tf_op jit(solution)/shard_map/ppermute | solution.py:25
  48.7 19.8 %collective-permute-start.3 = (bf16[4,1,1024]{0,2,1:T(8,128)(2,1)}, bf16[4,1,1024]{0,2,1:T(8,128)(2,1)S(1)}, u32[]{:S(2)}, u32[]{:S(2)}) collective-permute-start(bf16[4,1,1024]{0,2,1:T(8,128)(2,1)} %get-tuple-element.5), channel_id=1, source_target_pairs={{0,16},{4,20},{8,24},{12,28},{16,0},{20,4},{24,8},{28,12},{1,17},{... | collective-permute-start | bytes 24584 | tf_op jit(solution)/shard_map/ppermute | solution.py:25
  48.8 23.6 %collective-permute-start.4 = (bf16[4,1,1024]{0,2,1:T(8,128)(2,1)}, bf16[4,1,1024]{0,2,1:T(8,128)(2,1)S(1)}, u32[]{:S(2)}, u32[]{:S(2)}) collective-permute-start(bf16[4,1,1024]{0,2,1:T(8,128)(2,1)} %get-tuple-element.4), channel_id=1, source_target_pairs={{0,20},{4,16},{8,28},{12,24},{16,4},{20,0},{24,12},{28,8},{1,21},{... | collective-permute-start | bytes 24584 | tf_op jit(solution)/shard_map/ppermute | solution.py:25
  51.5 39.9 %collective-permute-start.5 = (bf16[4,1,1024]{0,2,1:T(8,128)(2,1)}, bf16[4,1,1024]{0,2,1:T(8,128)(2,1)S(1)}, u32[]{:S(2)}, u32[]{:S(2)}) collective-permute-start(bf16[4,1,1024]{0,2,1:T(8,128)(2,1)} %get-tuple-element.3), channel_id=1, source_target_pairs={{0,24},{4,28},{8,16},{12,20},{16,8},{20,12},{24,0},{28,4},{1,25},{... | collective-permute-start | bytes 24584 | tf_op jit(solution)/shard_map/ppermute | solution.py:25
  62.5 34.9 %collective-permute-start.6 = (bf16[4,1,1024]{0,2,1:T(8,128)(2,1)}, bf16[4,1,1024]{0,2,1:T(8,128)(2,1)S(1)}, u32[]{:S(2)}, u32[]{:S(2)}) collective-permute-start(bf16[4,1,1024]{0,2,1:T(8,128)(2,1)} %get-tuple-element.2), channel_id=1, source_target_pairs={{0,28},{4,24},{8,20},{12,16},{16,12},{20,8},{24,4},{28,0},{1,29},{... | collective-permute-start | bytes 24584 | tf_op jit(solution)/shard_map/ppermute | solution.py:25
Sparse Core Ops, SparseCore 0:
  24.5 26.1 reduce-scatter.1
